TPU v7x, 32 devices: a whole 2x2x4 slice. The times are simulated.
32 devices in a mesh: corpus: 4 (over y, x), fsdp: 8 (over z, core).
Axes of the slice: x: 2, y: 2, z: 4, core: 2. Of those that a mesh axis runs over, the one named last changes fastest.
Arguments:
- inputs: bfloat16 [2048, 4096], P('fsdp', 'corpus'), may hold values from -128 to 128
- norm_gain: float32 [4096], replicated, may hold values from 0.1 to 1.9
- w_query: bfloat16 [4096, 8192], P('fsdp', 'corpus'), may hold values from -0.09375 to 0.09375
- w_key: bfloat16 [4096, 1024], P('fsdp', 'corpus'), may hold values from -0.09375 to 0.09375
- w_value: bfloat16 [4096, 1024], P('fsdp', 'corpus'), may hold values from -0.375 to 0.375
- query_bias: float32 [8192], P('corpus'), may hold values from -16 to 16
- key_bias: float32 [1024], P('corpus'), may hold values from -16 to 16
- value_bias: float32 [1024], P('corpus'), may hold values from -4 to 4
- key_cache: bfloat16 [8, 2048, 1024], P('fsdp', None, 'corpus'), may hold values from -16 to 16
- value_cache: bfloat16 [8, 2048, 1024], P('fsdp', None, 'corpus'), may hold values from -16 to 16
- source_doc: int32 [32], P('fsdp'), may hold values from 0 to 7, as said below
- prefix_len: int32 [32], P('fsdp'), may hold values from 1 to 2048
Outputs:
- attention: bfloat16 [2048, 8192], P('fsdp', 'corpus')
Inputs may be any that keep to these rules, and one draw needn't show every extreme that they name: `source_doc`: within the suffixes of one index of fsdp (aligned blocks of 4) no document appears more than 2 times, and one document, drawn from the seed, appears exactly 2 times in every such block.
All inputs are finite; a program needn't handle non-finite values.
Results may differ from a plain program's by a relative error of at most 0.0075.
The roundings to bfloat16 on the way count: a program that leaves them out, or rounds other values in their place, can miss the bound.
Values may be sent and summed in bfloat16 or wider, within the bound.
A program may use at most 128 MiB of HBM per device.

v0:
```python
import jax
import jax.numpy as jnp
from jax import lax
from jax.sharding import PartitionSpec as P

HD = 128
SL = 64
CAP = 2
EPS = 1e-06
THETA = 1000000.0
MASKED = -1e30


def rope_tables(position, width):
    half = width // 2
    freq = THETA ** (-(jnp.arange(half, dtype=jnp.float32) * 2.0 / width))
    angle = position.astype(jnp.float32)[..., None] * freq
    angle = jnp.concatenate([angle, angle], axis=-1)
    return (jnp.cos(angle), jnp.sin(angle))


def rotate(vector, cosine, sine):
    half = vector.shape[-1] // 2
    turned = jnp.concatenate([-vector[..., half:], vector[..., :half]], axis=-1)
    return vector * cosine + turned * sine


def normalize(rows, norm_gain):
    wide = rows.astype(jnp.float32)
    spread = jnp.mean(wide * wide, axis=-1, keepdims=True)
    return (wide * lax.rsqrt(spread + EPS) * norm_gain).astype(jnp.bfloat16)


def partial_attend(query, keys, values, live):
    count = query.shape[0]
    width = query.shape[2]
    length = keys.shape[0]
    kv_heads = keys.shape[1] // width
    group = query.shape[1] // kv_heads
    grouped = query.reshape(count, kv_heads, group, width)
    key_rows = keys.reshape(length, kv_heads, width)
    scores = jnp.einsum(
        "tkgd,lkd->tkgl", grouped, key_rows, preferred_element_type=jnp.float32
    ) * width ** (-0.5)
    scores = jnp.where(live[:, None, None, :], scores, MASKED)
    peak = jnp.max(scores, axis=-1)
    weights = jnp.exp(scores - peak[..., None])
    total = jnp.sum(weights, axis=-1)
    rounded = weights.astype(jnp.bfloat16)
    value_rows = values.reshape(length, kv_heads, width)
    weighted = jnp.einsum("tkgl,lkd->tkgd", rounded, value_rows, preferred_element_type=jnp.float32)
    return (
        weighted.reshape(count, kv_heads * group * width),
        peak.reshape(count, kv_heads * group),
        total.reshape(count, kv_heads * group),
    )


def settle(part):
    weighted, peak, total = part
    shape = peak.shape + (-1,)
    normed = (
        (weighted.reshape(shape) / total[..., None]).reshape(weighted.shape).astype(jnp.bfloat16)
    )
    return (normed, peak + jnp.log(total))


def combine(prefix_normed, prefix_lse, own):
    own_out, own_peak, own_total = own
    top = jnp.maximum(prefix_lse, own_peak)
    scale_first = jnp.exp(prefix_lse - top)
    scale_second = jnp.exp(own_peak - top)
    divisor = scale_first + own_total * scale_second
    shape = own_peak.shape + (-1,)
    mixed = (
        prefix_normed.astype(jnp.float32).reshape(shape) * scale_first[..., None]
        + own_out.reshape(shape) * scale_second[..., None]
    )
    mixed = mixed / divisor[..., None]
    return mixed.reshape(own_peak.shape[:-1] + (-1,)).astype(jnp.bfloat16)


def shards(
    inputs,
    norm_gain,
    w_query,
    w_key,
    w_value,
    query_bias,
    key_bias,
    value_bias,
    key_cache,
    value_cache,
    source_doc,
    prefix_len,
):
    full_rows = lax.all_gather(inputs, "corpus", axis=1, tiled=True)
    normed = normalize(full_rows, norm_gain)
    query_lin = jnp.dot(
        normed,
        lax.all_gather(w_query, "fsdp", axis=0, tiled=True),
        preferred_element_type=jnp.float32,
    )
    key_lin = jnp.dot(
        normed,
        lax.all_gather(w_key, "fsdp", axis=0, tiled=True),
        preferred_element_type=jnp.float32,
    )
    value_lin = jnp.dot(
        normed,
        lax.all_gather(w_value, "fsdp", axis=0, tiled=True),
        preferred_element_type=jnp.float32,
    )
    suffixes = source_doc.shape[0]
    width = HD
    q_heads = w_query.shape[1] // width
    kv_heads = w_key.shape[1] // width
    position = prefix_len[:, None] + jnp.arange(SL, dtype=jnp.int32)[None, :]
    cosine, sine = rope_tables(position, width)
    cosine = cosine[:, :, None, :]
    sine = sine[:, :, None, :]
    queries = rotate(
        (query_lin + query_bias).reshape(suffixes, SL, q_heads, width), cosine, sine
    ).astype(jnp.bfloat16)
    own_keys = rotate(
        (key_lin + key_bias).reshape(suffixes, SL, kv_heads, width), cosine, sine
    ).astype(jnp.bfloat16)
    own_keys = own_keys.reshape(suffixes, SL, kv_heads * width)
    own_values = (
        (value_lin + value_bias).astype(jnp.bfloat16).reshape(suffixes, SL, kv_heads * width)
    )
    causal = jnp.arange(SL, dtype=jnp.int32)[None, :] <= jnp.arange(SL, dtype=jnp.int32)[:, None]
    own_part = jax.vmap(partial_attend, in_axes=(0, 0, 0, None))(
        queries, own_keys, own_values, causal
    )
    documents = lax.axis_size("fsdp")
    slots = documents * CAP
    doc_length = key_cache.shape[1]
    order = jnp.arange(suffixes, dtype=jnp.int32)
    earlier = (source_doc[None, :] == source_doc[:, None]) & (order[None, :] < order[:, None])
    ranking = jnp.sum(earlier.astype(jnp.int32), axis=1)
    slot_of = source_doc * CAP + ranking
    matches = slot_of[None, :] == jnp.arange(slots, dtype=jnp.int32)[:, None]
    holder = jnp.sum(jnp.where(matches, order[None, :], 0), axis=1)
    occupied = jnp.any(matches, axis=1)
    slot_length = jnp.where(occupied, jnp.take(prefix_len, holder, axis=0), 0)
    slot_mask = (jnp.arange(doc_length, dtype=jnp.int32)[None, :] < slot_length[:, None]).astype(
        jnp.bfloat16
    )
    slot_queries = jnp.take(queries, holder, axis=0)
    initial = (
        jnp.zeros((suffixes, SL, q_heads * width), jnp.float32),
        jnp.zeros((suffixes, SL, q_heads), jnp.float32),
        jnp.zeros((suffixes, SL, q_heads), jnp.float32),
    )
    key_piece = lax.all_gather(key_cache, "fsdp", axis=0, tiled=True)
    value_piece = lax.all_gather(value_cache, "fsdp", axis=0, tiled=True)
    count = key_piece.shape[0]

    def one_document(item):
        doc_queries, doc_masks, doc_keys, doc_values = item
        live = jnp.broadcast_to(doc_masks[:, None, :] > 0, (CAP, SL, doc_masks.shape[-1]))
        return jax.vmap(partial_attend, in_axes=(0, None, None, 0))(
            doc_queries, doc_keys, doc_values, live
        )

    results = lax.map(
        one_document,
        (
            slot_queries.reshape((count, CAP) + slot_queries.shape[1:]),
            slot_mask.reshape(count, CAP, doc_length),
            key_piece,
            value_piece,
        ),
    )
    results = tuple((part.reshape((count * CAP,) + part.shape[2:]) for part in results))
    inside = (slot_of >= 0) & (slot_of < count * CAP)
    chosen = jnp.clip(slot_of, 0, count * CAP - 1)
    gathered_part = tuple(
        (
            jnp.where(inside[:, None, None], jnp.take(fresh, chosen, axis=0), older)
            for older, fresh in zip(initial, results)
        )
    )
    prefix_normed, prefix_lse = settle(gathered_part)
    attention = combine(prefix_normed, prefix_lse, own_part)
    return attention.reshape(suffixes * SL, q_heads * width)


def solution(mesh):
    in_specs = (
        P("fsdp", "corpus"),
        P(),
        P("fsdp", "corpus"),
        P("fsdp", "corpus"),
        P("fsdp", "corpus"),
        P("corpus"),
        P("corpus"),
        P("corpus"),
        P("fsdp", None, "corpus"),
        P("fsdp", None, "corpus"),
        P("fsdp"),
        P("fsdp"),
    )
    out_specs = P("fsdp", "corpus")
    return jax.shard_map(shards, mesh=mesh, in_specs=in_specs, out_specs=out_specs, check_vma=False)
```

profile of v0, /device:TPU:0, one launch (start us, length us, event | category | flops | bytes accessed | tf_op | source)
XLA Modules:
  0.0 685.7 jit_solution(6007420988527938023)
XLA Ops:
  15.4 31.9 %all-gather.11.cloned.1.call-done = bf16[256,4096]{1,0:T(8,128)(2,1)} async-done(((bf16[256,1024]{1,0:T(8,128)(2,1)}), bf16[256,4096]{1,0:T(8,128)(2,1)}) %all-gather.11.cloned.1.call-update) | async-done | bytes 2097168 | tf_op jit(solution)/shard_map/all_gather | solution.py:97
  47.3 2.2 fusion.13
  49.5 28.5 %all-gather.15.cloned.1.call-done = bf16[4096,256]{1,0:T(8,128)(2,1)} async-done(((bf16[512,256]{1,0:T(8,128)(2,1)}), bf16[4096,256]{1,0:T(8,128)(2,1)}) %all-gather.15.cloned.1.call-update) | async-done | bytes 2097168 | tf_op jit(solution)/shard_map/all_gather | solution.py:106
  78.0 2.4 convolution_add_fusion.2
  80.5 27.7 %all-gather.17.cloned.1.call-done = bf16[4096,256]{1,0:T(8,128)(2,1)} async-done(((bf16[512,256]{1,0:T(8,128)(2,1)}), bf16[4096,256]{1,0:T(8,128)(2,1)}) %all-gather.17.cloned.1.call-update) | async-done | bytes 2097168 | tf_op jit(solution)/shard_map/all_gather | solution.py:111
  108.2 2.4 fusion.27
  110.8 149.5 %all-gather.13.cloned.1.call-done = bf16[4096,2048]{1,0:T(8,128)(2,1)} async-done(((bf16[512,2048]{1,0:T(8,128)(2,1)}), bf16[4096,2048]{1,0:T(8,128)(2,1)}) %all-gather.13.cloned.1.call-update) | async-done | bytes 16777232 | tf_op jit(solution)/shard_map/all_gather | solution.py:101
  260.3 8.2 %fusion.26 = f32[32,8,16,128]{3,1,2,0:T(8,128)S(1)} fusion(bf16[4096,2048]{1,0:T(8,128)(2,1)} %all-gather.13.cloned.1.call-done, f32[2048]{0:T(1024)S(1)} %copy-done.18, bf16[256,4096]{1,0:T(8,128)(2,1)S(1)} %copy-done.7, f32[4096]{0:T(1024)S(1)} %copy-done.17, f32[256]{0:T(256)S(1)} %add_rsqrt_fusion), kind=kOutput, calls=%fused_computation.52 | convolution fusion | flops 4299685888 | bytes 20997120 | tf_op jit(solution)/shard_map/dot_general | solution.py:99
  272.3 1.6 fusion.56
  275.3 2.5 copy.105
  277.8 2.7 reshape.216
  280.5 3.0 fusion.20
  283.5 3.0 gather_fusion.1
  287.0 4.6 broadcast_select_fusion
  291.7 50.4 %all-gather.9.cloned.1.call-done = bf16[8,2048,256]{2,1,0:T(8,128)(2,1)} async-done(((bf16[1,2048,256]{2,1,0:T(8,128)(2,1)}), bf16[8,2048,256]{2,1,0:T(8,128)(2,1)}) %all-gather.9.cloned.1.call-update) | async-done | bytes 8388624 | tf_op jit(solution)/shard_map/all_gather | solution.py:156
  342.1 82.1 %all-gather.7.cloned.1.call-done = bf16[8,2048,256]{2,1,0:T(8,128)(2,1)} async-done(((bf16[1,2048,256]{2,1,0:T(8,128)(2,1)}), bf16[8,2048,256]{2,1,0:T(8,128)(2,1)}) %all-gather.7.cloned.1.call-update) | async-done | bytes 8388624 | tf_op jit(solution)/shard_map/all_gather | solution.py:157
  424.2 241.4 %while.14 = (s32[]{:T(128)}, f32[8,2,64,2048]{3,2,1,0:T(8,128)}, f32[8,2,64,16]{2,3,1,0:T(8,128)S(1)}, f32[8,2,64,16]{2,3,1,0:T(8,128)S(1)}, bf16[8,2048,256]{2,...) while((s32[]{:T(128)}, f32[8,2,64,2048]{3,2,1,0:T(8,128)}, ...), condition=%wide.region_7.8_spmd, body=%wide.region_4.0_spmd.sunk | while | flops 2193620992 | bytes 74047632 | solution.py:167
  428.5 1.4 copy.160
  429.9 7.1 %fusion.71 = (f32[2,64,2,8]{1,3,0,2:T(8,128)S(1)}, f32[2,2048,2,64,8]{1,3,4,2,0:T(8,128)}) fusion(pred[2,2048]{1,0:T(4,128)(4,1)S(1)} %compare_bitcast_fusion.2, bf16[2048,2,128,1,1]{0,2,4,3,1:T(8,128)(2,1)S(1)} %bitcast.138, bf16[2,64,2,8,128]{4,3,2,1,0:T(8,128)(2,1)S(1)} %dynamic-slice_bitcast_fusion.2), kind=kOutput, calls=%fused_computation.9.clone.1 | convolution fusion | flops 1086322688 | bytes 18362368 | tf_op jit(solution)/shard_map/while/body/eval_jaxpr/vmap(tkgd,lkd->tkgl)/dot_general | solution.py:42
  437.1 7.6 %fusion.72 = f32[2,64,2,8,128]{4,1,3,0,2:T(8,128)S(1)} fusion(bf16[2048,2,128,1,1]{0,2,4,3,1:T(8,128)(2,1)S(1)} %bitcast.142, f32[2,2048,2,64,8]{1,3,4,2,0:T(8,128)} %get-tuple-element.168, f32[2,64,2,8]{1,3,0,2:T(8,128)S(1)} %get-tuple-element.169, pred[2,2048]{1,0:T(4,128)(4,1)S(1)} %compare_bitcast_fusion.2), kind=kOutput, calls=%fused_computation.12.clone.1 | convolution fusion | flops 1090519040 | bytes 18886656 | tf_op jit(solution)/shard_map/while/body/eval_jaxpr/vmap(tkgl,lkd->tkgd)/dot_general | solution.py:51
  444.6 7.8 %fusion.73 = f32[2,64,2,8]{1,3,0,2:T(8,128)S(1)} fusion(f32[2,2048,2,64,8]{1,3,4,2,0:T(8,128)} %get-tuple-element.168, f32[2,64,2,8]{1,3,0,2:T(8,128)S(1)} %get-tuple-element.169, pred[2,2048]{1,0:T(4,128)(4,1)S(1)} %compare_bitcast_fusion.2), kind=kLoop, calls=%fused_computation.7.clone.1 | loop fusion | flops 16775168 | bytes 16797696 | tf_op jit(solution)/shard_map/while/body/eval_jaxpr/vmap()/reduce_sum | solution.py:48
  460.1 7.1 %fusion.71 = (f32[2,64,2,8]{1,3,0,2:T(8,128)S(1)}, f32[2,2048,2,64,8]{1,3,4,2,0:T(8,128)}) fusion(pred[2,2048]{1,0:T(4,128)(4,1)S(1)} %compare_bitcast_fusion.2, bf16[2048,2,128,1,1]{0,2,4,3,1:T(8,128)(2,1)S(1)} %bitcast.138, bf16[2,64,2,8,128]{4,3,2,1,0:T(8,128)(2,1)S(1)} %dynamic-slice_bitcast_fusion.2), kind=kOutput, calls=%fused_computation.9.clone.1 | convolution fusion | flops 1086322688 | bytes 18362368 | tf_op jit(solution)/shard_map/while/body/eval_jaxpr/vmap(tkgd,lkd->tkgl)/dot_general | solution.py:42
  467.2 7.6 %fusion.72 = f32[2,64,2,8,128]{4,1,3,0,2:T(8,128)S(1)} fusion(bf16[2048,2,128,1,1]{0,2,4,3,1:T(8,128)(2,1)S(1)} %bitcast.142, f32[2,2048,2,64,8]{1,3,4,2,0:T(8,128)} %get-tuple-element.168, f32[2,64,2,8]{1,3,0,2:T(8,128)S(1)} %get-tuple-element.169, pred[2,2048]{1,0:T(4,128)(4,1)S(1)} %compare_bitcast_fusion.2), kind=kOutput, calls=%fused_computation.12.clone.1 | convolution fusion | flops 1090519040 | bytes 18886656 | tf_op jit(solution)/shard_map/while/body/eval_jaxpr/vmap(tkgl,lkd->tkgd)/dot_general | solution.py:51
  474.8 7.8 %fusion.73 = f32[2,64,2,8]{1,3,0,2:T(8,128)S(1)} fusion(f32[2,2048,2,64,8]{1,3,4,2,0:T(8,128)} %get-tuple-element.168, f32[2,64,2,8]{1,3,0,2:T(8,128)S(1)} %get-tuple-element.169, pred[2,2048]{1,0:T(4,128)(4,1)S(1)} %compare_bitcast_fusion.2), kind=kLoop, calls=%fused_computation.7.clone.1 | loop fusion | flops 16775168 | bytes 16797696 | tf_op jit(solution)/shard_map/while/body/eval_jaxpr/vmap()/reduce_sum | solution.py:48
  488.8 1.4 copy.160
  490.3 7.1 %fusion.71 = (f32[2,64,2,8]{1,3,0,2:T(8,128)S(1)}, f32[2,2048,2,64,8]{1,3,4,2,0:T(8,128)}) fusion(pred[2,2048]{1,0:T(4,128)(4,1)S(1)} %compare_bitcast_fusion.2, bf16[2048,2,128,1,1]{0,2,4,3,1:T(8,128)(2,1)S(1)} %bitcast.138, bf16[2,64,2,8,128]{4,3,2,1,0:T(8,128)(2,1)S(1)} %dynamic-slice_bitcast_fusion.2), kind=kOutput, calls=%fused_computation.9.clone.1 | convolution fusion | flops 1086322688 | bytes 18362368 | tf_op jit(solution)/shard_map/while/body/eval_jaxpr/vmap(tkgd,lkd->tkgl)/dot_general | solution.py:42
  497.4 7.6 %fusion.72 = f32[2,64,2,8,128]{4,1,3,0,2:T(8,128)S(1)} fusion(bf16[2048,2,128,1,1]{0,2,4,3,1:T(8,128)(2,1)S(1)} %bitcast.142, f32[2,2048,2,64,8]{1,3,4,2,0:T(8,128)} %get-tuple-element.168, f32[2,64,2,8]{1,3,0,2:T(8,128)S(1)} %get-tuple-element.169, pred[2,2048]{1,0:T(4,128)(4,1)S(1)} %compare_bitcast_fusion.2), kind=kOutput, calls=%fused_computation.12.clone.1 | convolution fusion | flops 1090519040 | bytes 18886656 | tf_op jit(solution)/shard_map/while/body/eval_jaxpr/vmap(tkgl,lkd->tkgd)/dot_general | solution.py:51
  505.0 7.8 %fusion.73 = f32[2,64,2,8]{1,3,0,2:T(8,128)S(1)} fusion(f32[2,2048,2,64,8]{1,3,4,2,0:T(8,128)} %get-tuple-element.168, f32[2,64,2,8]{1,3,0,2:T(8,128)S(1)} %get-tuple-element.169, pred[2,2048]{1,0:T(4,128)(4,1)S(1)} %compare_bitcast_fusion.2), kind=kLoop, calls=%fused_computation.7.clone.1 | loop fusion | flops 16775168 | bytes 16797696 | tf_op jit(solution)/shard_map/while/body/eval_jaxpr/vmap()/reduce_sum | solution.py:48
  519.0 1.4 copy.160
  520.4 7.1 %fusion.71 = (f32[2,64,2,8]{1,3,0,2:T(8,128)S(1)}, f32[2,2048,2,64,8]{1,3,4,2,0:T(8,128)}) fusion(pred[2,2048]{1,0:T(4,128)(4,1)S(1)} %compare_bitcast_fusion.2, bf16[2048,2,128,1,1]{0,2,4,3,1:T(8,128)(2,1)S(1)} %bitcast.138, bf16[2,64,2,8,128]{4,3,2,1,0:T(8,128)(2,1)S(1)} %dynamic-slice_bitcast_fusion.2), kind=kOutput, calls=%fused_computation.9.clone.1 | convolution fusion | flops 1086322688 | bytes 18362368 | tf_op jit(solution)/shard_map/while/body/eval_jaxpr/vmap(tkgd,lkd->tkgl)/dot_general | solution.py:42
  527.6 7.6 %fusion.72 = f32[2,64,2,8,128]{4,1,3,0,2:T(8,128)S(1)} fusion(bf16[2048,2,128,1,1]{0,2,4,3,1:T(8,128)(2,1)S(1)} %bitcast.142, f32[2,2048,2,64,8]{1,3,4,2,0:T(8,128)} %get-tuple-element.168, f32[2,64,2,8]{1,3,0,2:T(8,128)S(1)} %get-tuple-element.169, pred[2,2048]{1,0:T(4,128)(4,1)S(1)} %compare_bitcast_fusion.2), kind=kOutput, calls=%fused_computation.12.clone.1 | convolution fusion | flops 1090519040 | bytes 18886656 | tf_op jit(solution)/shard_map/while/body/eval_jaxpr/vmap(tkgl,lkd->tkgd)/dot_general | solution.py:51
  535.1 7.8 %fusion.73 = f32[2,64,2,8]{1,3,0,2:T(8,128)S(1)} fusion(f32[2,2048,2,64,8]{1,3,4,2,0:T(8,128)} %get-tuple-element.168, f32[2,64,2,8]{1,3,0,2:T(8,128)S(1)} %get-tuple-element.169, pred[2,2048]{1,0:T(4,128)(4,1)S(1)} %compare_bitcast_fusion.2), kind=kLoop, calls=%fused_computation.7.clone.1 | loop fusion | flops 16775168 | bytes 16797696 | tf_op jit(solution)/shard_map/while/body/eval_jaxpr/vmap()/reduce_sum | solution.py:48
  550.6 7.1 %fusion.71 = (f32[2,64,2,8]{1,3,0,2:T(8,128)S(1)}, f32[2,2048,2,64,8]{1,3,4,2,0:T(8,128)}) fusion(pred[2,2048]{1,0:T(4,128)(4,1)S(1)} %compare_bitcast_fusion.2, bf16[2048,2,128,1,1]{0,2,4,3,1:T(8,128)(2,1)S(1)} %bitcast.138, bf16[2,64,2,8,128]{4,3,2,1,0:T(8,128)(2,1)S(1)} %dynamic-slice_bitcast_fusion.2), kind=kOutput, calls=%fused_computation.9.clone.1 | convolution fusion | flops 1086322688 | bytes 18362368 | tf_op jit(solution)/shard_map/while/body/eval_jaxpr/vmap(tkgd,lkd->tkgl)/dot_general | solution.py:42
  557.7 7.6 %fusion.72 = f32[2,64,2,8,128]{4,1,3,0,2:T(8,128)S(1)} fusion(bf16[2048,2,128,1,1]{0,2,4,3,1:T(8,128)(2,1)S(1)} %bitcast.142, f32[2,2048,2,64,8]{1,3,4,2,0:T(8,128)} %get-tuple-element.168, f32[2,64,2,8]{1,3,0,2:T(8,128)S(1)} %get-tuple-element.169, pred[2,2048]{1,0:T(4,128)(4,1)S(1)} %compare_bitcast_fusion.2), kind=kOutput, calls=%fused_computation.12.clone.1 | convolution fusion | flops 1090519040 | bytes 18886656 | tf_op jit(solution)/shard_map/while/body/eval_jaxpr/vmap(tkgl,lkd->tkgd)/dot_general | solution.py:51
  565.3 7.8 %fusion.73 = f32[2,64,2,8]{1,3,0,2:T(8,128)S(1)} fusion(f32[2,2048,2,64,8]{1,3,4,2,0:T(8,128)} %get-tuple-element.168, f32[2,64,2,8]{1,3,0,2:T(8,128)S(1)} %get-tuple-element.169, pred[2,2048]{1,0:T(4,128)(4,1)S(1)} %compare_bitcast_fusion.2), kind=kLoop, calls=%fused_computation.7.clone.1 | loop fusion | flops 16775168 | bytes 16797696 | tf_op jit(solution)/shard_map/while/body/eval_jaxpr/vmap()/reduce_sum | solution.py:48
  579.4 1.4 copy.160
  580.8 7.1 %fusion.71 = (f32[2,64,2,8]{1,3,0,2:T(8,128)S(1)}, f32[2,2048,2,64,8]{1,3,4,2,0:T(8,128)}) fusion(pred[2,2048]{1,0:T(4,128)(4,1)S(1)} %compare_bitcast_fusion.2, bf16[2048,2,128,1,1]{0,2,4,3,1:T(8,128)(2,1)S(1)} %bitcast.138, bf16[2,64,2,8,128]{4,3,2,1,0:T(8,128)(2,1)S(1)} %dynamic-slice_bitcast_fusion.2), kind=kOutput, calls=%fused_computation.9.clone.1 | convolution fusion | flops 1086322688 | bytes 18362368 | tf_op jit(solution)/shard_map/while/body/eval_jaxpr/vmap(tkgd,lkd->tkgl)/dot_general | solution.py:42
  587.9 7.6 %fusion.72 = f32[2,64,2,8,128]{4,1,3,0,2:T(8,128)S(1)} fusion(bf16[2048,2,128,1,1]{0,2,4,3,1:T(8,128)(2,1)S(1)} %bitcast.142, f32[2,2048,2,64,8]{1,3,4,2,0:T(8,128)} %get-tuple-element.168, f32[2,64,2,8]{1,3,0,2:T(8,128)S(1)} %get-tuple-element.169, pred[2,2048]{1,0:T(4,128)(4,1)S(1)} %compare_bitcast_fusion.2), kind=kOutput, calls=%fused_computation.12.clone.1 | convolution fusion | flops 1090519040 | bytes 18886656 | tf_op jit(solution)/shard_map/while/body/eval_jaxpr/vmap(tkgl,lkd->tkgd)/dot_general | solution.py:51
  595.5 7.8 %fusion.73 = f32[2,64,2,8]{1,3,0,2:T(8,128)S(1)} fusion(f32[2,2048,2,64,8]{1,3,4,2,0:T(8,128)} %get-tuple-element.168, f32[2,64,2,8]{1,3,0,2:T(8,128)S(1)} %get-tuple-element.169, pred[2,2048]{1,0:T(4,128)(4,1)S(1)} %compare_bitcast_fusion.2), kind=kLoop, calls=%fused_computation.7.clone.1 | loop fusion | flops 16775168 | bytes 16797696 | tf_op jit(solution)/shard_map/while/body/eval_jaxpr/vmap()/reduce_sum | solution.py:48
  611.0 7.1 %fusion.71 = (f32[2,64,2,8]{1,3,0,2:T(8,128)S(1)}, f32[2,2048,2,64,8]{1,3,4,2,0:T(8,128)}) fusion(pred[2,2048]{1,0:T(4,128)(4,1)S(1)} %compare_bitcast_fusion.2, bf16[2048,2,128,1,1]{0,2,4,3,1:T(8,128)(2,1)S(1)} %bitcast.138, bf16[2,64,2,8,128]{4,3,2,1,0:T(8,128)(2,1)S(1)} %dynamic-slice_bitcast_fusion.2), kind=kOutput, calls=%fused_computation.9.clone.1 | convolution fusion | flops 1086322688 | bytes 18362368 | tf_op jit(solution)/shard_map/while/body/eval_jaxpr/vmap(tkgd,lkd->tkgl)/dot_general | solution.py:42
  618.1 7.6 %fusion.72 = f32[2,64,2,8,128]{4,1,3,0,2:T(8,128)S(1)} fusion(bf16[2048,2,128,1,1]{0,2,4,3,1:T(8,128)(2,1)S(1)} %bitcast.142, f32[2,2048,2,64,8]{1,3,4,2,0:T(8,128)} %get-tuple-element.168, f32[2,64,2,8]{1,3,0,2:T(8,128)S(1)} %get-tuple-element.169, pred[2,2048]{1,0:T(4,128)(4,1)S(1)} %compare_bitcast_fusion.2), kind=kOutput, calls=%fused_computation.12.clone.1 | convolution fusion | flops 1090519040 | bytes 18886656 | tf_op jit(solution)/shard_map/while/body/eval_jaxpr/vmap(tkgl,lkd->tkgd)/dot_general | solution.py:51
  625.7 7.8 %fusion.73 = f32[2,64,2,8]{1,3,0,2:T(8,128)S(1)} fusion(f32[2,2048,2,64,8]{1,3,4,2,0:T(8,128)} %get-tuple-element.168, f32[2,64,2,8]{1,3,0,2:T(8,128)S(1)} %get-tuple-element.169, pred[2,2048]{1,0:T(4,128)(4,1)S(1)} %compare_bitcast_fusion.2), kind=kLoop, calls=%fused_computation.7.clone.1 | loop fusion | flops 16775168 | bytes 16797696 | tf_op jit(solution)/shard_map/while/body/eval_jaxpr/vmap()/reduce_sum | solution.py:48
  639.7 1.4 copy.160
  641.1 7.1 %fusion.71 = (f32[2,64,2,8]{1,3,0,2:T(8,128)S(1)}, f32[2,2048,2,64,8]{1,3,4,2,0:T(8,128)}) fusion(pred[2,2048]{1,0:T(4,128)(4,1)S(1)} %compare_bitcast_fusion.2, bf16[2048,2,128,1,1]{0,2,4,3,1:T(8,128)(2,1)S(1)} %bitcast.138, bf16[2,64,2,8,128]{4,3,2,1,0:T(8,128)(2,1)S(1)} %dynamic-slice_bitcast_fusion.2), kind=kOutput, calls=%fused_computation.9.clone.1 | convolution fusion | flops 1086322688 | bytes 18362368 | tf_op jit(solution)/shard_map/while/body/eval_jaxpr/vmap(tkgd,lkd->tkgl)/dot_general | solution.py:42
  648.2 7.6 %fusion.72 = f32[2,64,2,8,128]{4,1,3,0,2:T(8,128)S(1)} fusion(bf16[2048,2,128,1,1]{0,2,4,3,1:T(8,128)(2,1)S(1)} %bitcast.142, f32[2,2048,2,64,8]{1,3,4,2,0:T(8,128)} %get-tuple-element.168, f32[2,64,2,8]{1,3,0,2:T(8,128)S(1)} %get-tuple-element.169, pred[2,2048]{1,0:T(4,128)(4,1)S(1)} %compare_bitcast_fusion.2), kind=kOutput, calls=%fused_computation.12.clone.1 | convolution fusion | flops 1090519040 | bytes 18886656 | tf_op jit(solution)/shard_map/while/body/eval_jaxpr/vmap(tkgl,lkd->tkgd)/dot_general | solution.py:51
  655.8 7.8 %fusion.73 = f32[2,64,2,8]{1,3,0,2:T(8,128)S(1)} fusion(f32[2,2048,2,64,8]{1,3,4,2,0:T(8,128)} %get-tuple-element.168, f32[2,64,2,8]{1,3,0,2:T(8,128)S(1)} %get-tuple-element.169, pred[2,2048]{1,0:T(4,128)(4,1)S(1)} %compare_bitcast_fusion.2), kind=kLoop, calls=%fused_computation.7.clone.1 | loop fusion | flops 16775168 | bytes 16797696 | tf_op jit(solution)/shard_map/while/body/eval_jaxpr/vmap()/reduce_sum | solution.py:48
  666.2 4.2 gather_fusion.2
  674.5 4.4 fusion.16
  (191 shorter events, 73.0 us)
Async XLA Ops:
  6.5 40.7 %all-gather.11.cloned.1.call-start = ((), (), s32[]{:S(2)}) async-start(), calls=%async_computation.2 | async-start | bytes 2621440 | tf_op jit(solution)/shard_map/all_gather | solution.py:97
  7.3 70.7 %all-gather.15.cloned.1.call-start = ((), (), s32[]{:S(2)}) async-start(), calls=%async_computation.4 | async-start | bytes 2359296 | tf_op jit(solution)/shard_map/all_gather | solution.py:106
  8.0 100.2 %all-gather.17.cloned.1.call-start = ((), (), s32[]{:S(2)}) async-start(), calls=%async_computation.5 | async-start | bytes 2359296 | tf_op jit(solution)/shard_map/all_gather | solution.py:111
  8.7 1.8 copy-start.16
  8.8 4.3 copy-start
  8.8 251.5 %all-gather.13.cloned.1.call-start = ((), (), s32[]{:S(2)}) async-start(), calls=%async_computation.3 | async-start | bytes 18874368 | tf_op jit(solution)/shard_map/all_gather | solution.py:101
  9.3 332.7 %all-gather.9.cloned.1.call-start = ((), (), s32[]{:S(2)}) async-start(), calls=%async_computation.1 | async-start | bytes 9437184 | tf_op jit(solution)/shard_map/all_gather | solution.py:156
  9.9 68.1 %copy-start.17 = (f32[4096]{0:T(1024)S(1)}, f32[4096]{0:T(1024)}, u32[]{:S(2)}) copy-start(f32[4096]{0:T(1024)} %param.17) | copy-start | bytes 49156
  9.9 68.1 %copy-start.19 = (f32[256]{0:T(256)S(1)}, f32[256]{0:T(256)}, u32[]{:S(2)}) copy-start(f32[256]{0:T(256)} %param.22) | copy-start | bytes 3076
  9.9 414.2 %all-gather.7.cloned.1.call-start = ((), (), s32[]{:S(2)}) async-start(), calls=%async_computation | async-start | bytes 9437184 | tf_op jit(solution)/shard_map/all_gather | solution.py:157
  10.8 0.5 copy-start.10
  12.2 3.2 copy-start.14
  47.3 30.7 %copy-start.7 = (bf16[256,4096]{1,0:T(8,128)(2,1)S(1)}, bf16[256,4096]{1,0:T(8,128)(2,1)}, u32[]{:S(2)}) copy-start(bf16[256,4096]{1,0:T(8,128)(2,1)} %all-gather.11.cloned.1.call-done) | copy-start | bytes 6291460
  49.5 58.7 %copy-start.20 = (f32[256]{0:T(256)S(1)}, f32[256]{0:T(256)}, u32[]{:S(2)}) copy-start(f32[256]{0:T(256)} %param.23) | copy-start | bytes 3076
  80.5 179.8 %copy-start.18 = (f32[2048]{0:T(1024)S(1)}, f32[2048]{0:T(1024)}, u32[]{:S(2)}) copy-start(f32[2048]{0:T(1024)} %param.21) | copy-start | bytes 24580
  269.6 1.3 copy-start.4
  269.6 2.0 copy-start.5
  273.9 1.4 copy-start.2
  283.5 3.0 copy-start.3
  287.0 137.1 %copy-start.8 = (f32[8,2,64,16]{2,3,1,0:T(8,128)S(1)}, f32[8,2,64,16]{2,3,1,0:T(8,128)}, u32[]{:S(2)}) copy-start(f32[8,2,64,16]{2,3,1,0:T(8,128)} %custom-call.12) | copy-start | bytes 196612
  287.0 137.1 %copy-start.9 = (f32[8,2,64,16]{2,3,1,0:T(8,128)S(1)}, f32[8,2,64,16]{2,3,1,0:T(8,128)}, u32[]{:S(2)}) copy-start(f32[8,2,64,16]{2,3,1,0:T(8,128)} %custom-call.11) | copy-start | bytes 196612
  429.9 7.1 %copy-start.1 = (bf16[1,2048,256]{1,2,0:T(8,128)(2,1)S(1)}, bf16[1,2048,256]{1,2,0:T(8,128)(2,1)}, u32[]{:S(2)}) copy-start(bf16[1,2048,256]{1,2,0:T(8,128)(2,1)} %copy.160) | copy-start | bytes 3145732 | tf_op jit(solution)/shard_map/while
  460.1 7.1 %copy-start.1 = (bf16[1,2048,256]{1,2,0:T(8,128)(2,1)S(1)}, bf16[1,2048,256]{1,2,0:T(8,128)(2,1)}, u32[]{:S(2)}) copy-start(bf16[1,2048,256]{1,2,0:T(8,128)(2,1)} %copy.160) | copy-start | bytes 3145732 | tf_op jit(solution)/shard_map/while
  490.3 7.1 %copy-start.1 = (bf16[1,2048,256]{1,2,0:T(8,128)(2,1)S(1)}, bf16[1,2048,256]{1,2,0:T(8,128)(2,1)}, u32[]{:S(2)}) copy-start(bf16[1,2048,256]{1,2,0:T(8,128)(2,1)} %copy.160) | copy-start | bytes 3145732 | tf_op jit(solution)/shard_map/while
  520.4 7.1 %copy-start.1 = (bf16[1,2048,256]{1,2,0:T(8,128)(2,1)S(1)}, bf16[1,2048,256]{1,2,0:T(8,128)(2,1)}, u32[]{:S(2)}) copy-start(bf16[1,2048,256]{1,2,0:T(8,128)(2,1)} %copy.160) | copy-start | bytes 3145732 | tf_op jit(solution)/shard_map/while
  550.6 7.1 %copy-start.1 = (bf16[1,2048,256]{1,2,0:T(8,128)(2,1)S(1)}, bf16[1,2048,256]{1,2,0:T(8,128)(2,1)}, u32[]{:S(2)}) copy-start(bf16[1,2048,256]{1,2,0:T(8,128)(2,1)} %copy.160) | copy-start | bytes 3145732 | tf_op jit(solution)/shard_map/while
  580.8 7.1 %copy-start.1 = (bf16[1,2048,256]{1,2,0:T(8,128)(2,1)S(1)}, bf16[1,2048,256]{1,2,0:T(8,128)(2,1)}, u32[]{:S(2)}) copy-start(bf16[1,2048,256]{1,2,0:T(8,128)(2,1)} %copy.160) | copy-start | bytes 3145732 | tf_op jit(solution)/shard_map/while
  611.0 7.1 %copy-start.1 = (bf16[1,2048,256]{1,2,0:T(8,128)(2,1)S(1)}, bf16[1,2048,256]{1,2,0:T(8,128)(2,1)}, u32[]{:S(2)}) copy-start(bf16[1,2048,256]{1,2,0:T(8,128)(2,1)} %copy.160) | copy-start | bytes 3145732 | tf_op jit(solution)/shard_map/while
  641.1 7.1 %copy-start.1 = (bf16[1,2048,256]{1,2,0:T(8,128)(2,1)S(1)}, bf16[1,2048,256]{1,2,0:T(8,128)(2,1)}, u32[]{:S(2)}) copy-start(bf16[1,2048,256]{1,2,0:T(8,128)(2,1)} %copy.160) | copy-start | bytes 3145732 | tf_op jit(solution)/shard_map/while
  666.2 4.9 copy-start.11
  666.2 4.9 copy-start.15
  672.9 1.6 copy-start.6
  672.9 1.6 copy-start.12
  672.9 1.6 copy-start.13
Sparse Core Ops, SparseCore 0:
  9.2 38.0 all-gather.10
  48.8 29.0 all-gather.14
  79.6 28.5 all-gather.16
  109.7 150.5 all-gather.12
  261.7 80.2 all-gather.8
  343.5 80.5 all-gather.6
where the time goes:
time: 687 us; the launch traced here: 686 us
  waiting for transfers between devices  374 us (54%)
  matrix products  133 us (19%)
  local copies, waits for them, and re-layouts  84.7 us (12%)
  other arithmetic  80.2 us (12%)
  between operations  13.9 us (2%)
    all_gather x1, waiting for transfers between devices, shards(): lax.all_gather(w_query, 'fsdp', axis=0, tiled=True)  150 us
    all_gather x1, waiting for transfers between devices, shards(): value_piece = lax.all_gather(value_cache, 'fsdp', axis=0, tiled=True)  82.1 us
    reduce_sum x9, other arithmetic, partial_attend(): total = jnp.sum(weights, axis=-1)  63 us
    dot_general x9, matrix products, partial_attend(): jnp.einsum('tkgl,lkd->tkgd', rounded, value_rows, preferred_element_type=...  61.1 us
    dot_general x9, matrix products, partial_attend(): jnp.einsum('tkgd,lkd->tkgl', grouped, key_rows, preferred_element_type=jn...  58.6 us
    all_gather x1, waiting for transfers between devices, shards(): key_piece = lax.all_gather(key_cache, 'fsdp', axis=0, tiled=True)  50.4 us
    dynamic_slice x32, local copies, waits for them, and re-layouts, shards(): lax.map(one_document, (slot_queries.reshape((count, CAP) + slot_queries.s...  37.3 us
    all_gather x1, waiting for transfers between devices, shards(): full_rows = lax.all_gather(inputs, 'corpus', axis=1, tiled=True)  31.9 us
  transfers between devices with their start and end apart: 6, of which 6 were waited for; matrix products, arithmetic and copies ran while one was open for 6% of the time, Pallas kernels for 0%

commit v1 on v0

--- a/solution.py
+++ b/solution.py
@@ -2,6 +2,7 @@
 import jax.numpy as jnp
 from jax import lax
 from jax.sharding import PartitionSpec as P
+from jax.lax import all_gather
 
 HD = 128
 SL = 64
@@ -9,6 +10,12 @@
 EPS = 1e-06
 THETA = 1000000.0
 MASKED = -1e30
+
+
+def supply_all_shelves_for(frame, raw):
+    back = all_gather(jnp.concatenate([frame, raw], axis=1), axis_name="fsdp", axis=0, tiled=True)
+    mat_out = jnp.split(back, [frame.shape[1]], axis=1)
+    return mat_out
 
 
 def rope_tables(position, width):
@@ -153,8 +160,7 @@
         jnp.zeros((suffixes, SL, q_heads), jnp.float32),
         jnp.zeros((suffixes, SL, q_heads), jnp.float32),
     )
-    key_piece = lax.all_gather(key_cache, "fsdp", axis=0, tiled=True)
-    value_piece = lax.all_gather(value_cache, "fsdp", axis=0, tiled=True)
+    key_piece, value_piece = supply_all_shelves_for(key_cache, value_cache)
     count = key_piece.shape[0]
 
     def one_document(item):

time: 687 us -> 686 us (level)
  waiting for transfers between devices: 374 us -> 358 us
  local copies, waits for them, and re-layouts: 84.7 us -> 97.1 us
    all_gather x2 -> x1, waiting for transfers between devices: 132 us -> 119 us  [supply_all_shelves_for(): all_gather(jnp.concatenate([frame, raw], axis=1), axis_name='fsdp', axis=...]
    split x0 -> x1, local copies, waits for them, and re-layouts: none -> 11.3 us  [supply_all_shelves_for(): mat_out = jnp.split(back, [frame.shape[1]], axis=1)]
  transfers between devices with their start and end apart: 6 -> 5, of which waited for: 6 -> 5; matrix products, arithmetic and copies ran while one was open for 6% -> 6% of each run, Pallas kernels for 0% -> 0%
where the time goes in v1:
time: 686 us; the launch traced here: 684 us
  waiting for transfers between devices  358 us (52%)
  matrix products  133 us (19%)
  local copies, waits for them, and re-layouts  97.1 us (14%)
  other arithmetic  81.6 us (12%)
  between operations  13.6 us (2%)
    all_gather x1, waiting for transfers between devices, shards(): lax.all_gather(w_query, 'fsdp', axis=0, tiled=True)  150 us
    all_gather x1, waiting for transfers between devices, supply_all_shelves_for(): all_gather(jnp.concatenate([frame, raw], axis=1), axis_name='fsdp', axis=...  119 us
    reduce_sum x9, other arithmetic, partial_attend(): total = jnp.sum(weights, axis=-1)  63 us
    dot_general x9, matrix products, partial_attend(): jnp.einsum('tkgl,lkd->tkgd', rounded, value_rows, preferred_element_type=...  61.1 us
    dot_general x9, matrix products, partial_attend(): jnp.einsum('tkgd,lkd->tkgl', grouped, key_rows, preferred_element_type=jn...  58.7 us
    dynamic_slice x32, local copies, waits for them, and re-layouts, shards(): lax.map(one_document, (slot_queries.reshape((count, CAP) + slot_queries.s...  37.3 us
    all_gather x1, waiting for transfers between devices, shards(): full_rows = lax.all_gather(inputs, 'corpus', axis=1, tiled=True)  30.9 us
    all_gather x1, waiting for transfers between devices, shards(): lax.all_gather(w_key, 'fsdp', axis=0, tiled=True)  28.5 us
  transfers between devices with their start and end apart: 5, of which 5 were waited for; matrix products, arithmetic and copies ran while one was open for 6% of the time, Pallas kernels for 0%

profile of v1, /device:TPU:0, one launch (start us, length us, event | category | flops | bytes accessed | tf_op | source)
XLA Modules:
  0.0 684.0 jit_solution(12089153393720007304)
XLA Ops:
  9.4 1.5 pad_maximum_fusion
  16.4 30.9 %all-gather.8.cloned.1.call-done = bf16[256,4096]{1,0:T(8,128)(2,1)} async-done(((bf16[256,1024]{1,0:T(8,128)(2,1)}), bf16[256,4096]{1,0:T(8,128)(2,1)}) %all-gather.8.cloned.1.call-update) | async-done | bytes 2097168 | tf_op jit(solution)/shard_map/all_gather | solution.py:104
  47.3 2.2 fusion.13
  49.5 28.5 %all-gather.12.cloned.1.call-done = bf16[4096,256]{1,0:T(8,128)(2,1)} async-done(((bf16[512,256]{1,0:T(8,128)(2,1)}), bf16[4096,256]{1,0:T(8,128)(2,1)}) %all-gather.12.cloned.1.call-update) | async-done | bytes 2097168 | tf_op jit(solution)/shard_map/all_gather | solution.py:113
  78.0 2.3 convolution_add_fusion.2
  80.5 27.7 %all-gather.14.cloned.1.call-done = bf16[4096,256]{1,0:T(8,128)(2,1)} async-done(((bf16[512,256]{1,0:T(8,128)(2,1)}), bf16[4096,256]{1,0:T(8,128)(2,1)}) %all-gather.14.cloned.1.call-update) | async-done | bytes 2097168 | tf_op jit(solution)/shard_map/all_gather | solution.py:118
  108.3 2.4 fusion.27
  110.8 149.5 %all-gather.10.cloned.1.call-done = bf16[4096,2048]{1,0:T(8,128)(2,1)} async-done(((bf16[512,2048]{1,0:T(8,128)(2,1)}), bf16[4096,2048]{1,0:T(8,128)(2,1)}) %all-gather.10.cloned.1.call-update) | async-done | bytes 16777232 | tf_op jit(solution)/shard_map/all_gather | solution.py:108
  260.4 8.2 %fusion.26 = f32[32,8,16,128]{3,1,2,0:T(8,128)S(1)} fusion(bf16[4096,2048]{1,0:T(8,128)(2,1)} %all-gather.10.cloned.1.call-done, f32[2048]{0:T(1024)S(1)} %copy-done.20, bf16[256,4096]{1,0:T(8,128)(2,1)S(1)} %copy-done.7, f32[4096]{0:T(1024)S(1)} %copy-done.19, f32[256]{0:T(256)S(1)} %add_rsqrt_fusion), kind=kOutput, calls=%fused_computation.53 | convolution fusion | flops 4299685888 | bytes 20997120 | tf_op jit(solution)/shard_map/dot_general | solution.py:106
  272.6 1.7 fusion.57
  275.7 2.5 copy.105
  278.2 2.8 reshape.216
  281.0 2.9 fusion.20
  283.9 3.0 gather_fusion.1
  287.5 4.6 broadcast_select_fusion
  292.1 119.1 %all-gather.6.cloned.1.call-done = bf16[8,4096,256]{2,1,0:T(8,128)(2,1)} async-done(((bf16[1,4096,256]{2,1,0:T(8,128)(2,1)}), bf16[8,4096,256]{2,1,0:T(8,128)(2,1)}) %all-gather.6.cloned.1.call-update) | async-done | bytes 16777232 | tf_op jit(solution)/shard_map/all_gather | solution.py:16
  411.2 11.3 %fusion.56 = (bf16[8,2048,256]{2,1,0:T(8,128)(2,1)}, bf16[8,2048,256]{2,1,0:T(8,128)(2,1)}) fusion(bf16[8,4096,256]{2,1,0:T(8,128)(2,1)} %all-gather.6.cloned.1.call-done), kind=kLoop, calls=%fused_computation.106 | loop fusion | bytes 33554432 | tf_op jit(solution)/shard_map/split | solution.py:17
  422.5 241.6 %while.14 = (s32[]{:T(128)}, f32[8,2,64,2048]{3,2,1,0:T(8,128)}, f32[8,2,64,16]{2,3,1,0:T(8,128)S(1)}, f32[8,2,64,16]{2,3,1,0:T(8,128)S(1)}, bf16[8,2048,256]{2,...) while((s32[]{:T(128)}, f32[8,2,64,2048]{3,2,1,0:T(8,128)}, ...), condition=%wide.region_7.8_spmd, body=%wide.region_4.0_spmd.sunk | while | flops 2193620992 | bytes 74047632 | solution.py:173
  427.1 1.4 copy.160
  428.5 7.1 %fusion.72 = (f32[2,64,2,8]{1,3,0,2:T(8,128)S(1)}, f32[2,2048,2,64,8]{1,3,4,2,0:T(8,128)}) fusion(pred[2,2048]{1,0:T(4,128)(4,1)S(1)} %compare_bitcast_fusion.2, bf16[2048,2,128,1,1]{0,2,4,3,1:T(8,128)(2,1)S(1)} %bitcast.138, bf16[2,64,2,8,128]{4,3,2,1,0:T(8,128)(2,1)S(1)} %dynamic-slice_bitcast_fusion.2), kind=kOutput, calls=%fused_computation.9.clone.1 | convolution fusion | flops 1086322688 | bytes 18362368 | tf_op jit(solution)/shard_map/while/body/eval_jaxpr/vmap(tkgd,lkd->tkgl)/dot_general | solution.py:49
  435.7 7.6 %fusion.73 = f32[2,64,2,8,128]{4,1,3,0,2:T(8,128)S(1)} fusion(bf16[2048,2,128,1,1]{0,2,4,3,1:T(8,128)(2,1)S(1)} %bitcast.142, f32[2,2048,2,64,8]{1,3,4,2,0:T(8,128)} %get-tuple-element.170, f32[2,64,2,8]{1,3,0,2:T(8,128)S(1)} %get-tuple-element.171, pred[2,2048]{1,0:T(4,128)(4,1)S(1)} %compare_bitcast_fusion.2), kind=kOutput, calls=%fused_computation.12.clone.1 | convolution fusion | flops 1090519040 | bytes 18886656 | tf_op jit(solution)/shard_map/while/body/eval_jaxpr/vmap(tkgl,lkd->tkgd)/dot_general | solution.py:58
  443.2 7.8 %fusion.74 = f32[2,64,2,8]{1,3,0,2:T(8,128)S(1)} fusion(f32[2,2048,2,64,8]{1,3,4,2,0:T(8,128)} %get-tuple-element.170, f32[2,64,2,8]{1,3,0,2:T(8,128)S(1)} %get-tuple-element.171, pred[2,2048]{1,0:T(4,128)(4,1)S(1)} %compare_bitcast_fusion.2), kind=kLoop, calls=%fused_computation.7.clone.1 | loop fusion | flops 16775168 | bytes 16797696 | tf_op jit(solution)/shard_map/while/body/eval_jaxpr/vmap()/reduce_sum | solution.py:55
  458.7 7.1 %fusion.72 = (f32[2,64,2,8]{1,3,0,2:T(8,128)S(1)}, f32[2,2048,2,64,8]{1,3,4,2,0:T(8,128)}) fusion(pred[2,2048]{1,0:T(4,128)(4,1)S(1)} %compare_bitcast_fusion.2, bf16[2048,2,128,1,1]{0,2,4,3,1:T(8,128)(2,1)S(1)} %bitcast.138, bf16[2,64,2,8,128]{4,3,2,1,0:T(8,128)(2,1)S(1)} %dynamic-slice_bitcast_fusion.2), kind=kOutput, calls=%fused_computation.9.clone.1 | convolution fusion | flops 1086322688 | bytes 18362368 | tf_op jit(solution)/shard_map/while/body/eval_jaxpr/vmap(tkgd,lkd->tkgl)/dot_general | solution.py:49
  465.8 7.6 %fusion.73 = f32[2,64,2,8,128]{4,1,3,0,2:T(8,128)S(1)} fusion(bf16[2048,2,128,1,1]{0,2,4,3,1:T(8,128)(2,1)S(1)} %bitcast.142, f32[2,2048,2,64,8]{1,3,4,2,0:T(8,128)} %get-tuple-element.170, f32[2,64,2,8]{1,3,0,2:T(8,128)S(1)} %get-tuple-element.171, pred[2,2048]{1,0:T(4,128)(4,1)S(1)} %compare_bitcast_fusion.2), kind=kOutput, calls=%fused_computation.12.clone.1 | convolution fusion | flops 1090519040 | bytes 18886656 | tf_op jit(solution)/shard_map/while/body/eval_jaxpr/vmap(tkgl,lkd->tkgd)/dot_general | solution.py:58
  473.4 7.8 %fusion.74 = f32[2,64,2,8]{1,3,0,2:T(8,128)S(1)} fusion(f32[2,2048,2,64,8]{1,3,4,2,0:T(8,128)} %get-tuple-element.170, f32[2,64,2,8]{1,3,0,2:T(8,128)S(1)} %get-tuple-element.171, pred[2,2048]{1,0:T(4,128)(4,1)S(1)} %compare_bitcast_fusion.2), kind=kLoop, calls=%fused_computation.7.clone.1 | loop fusion | flops 16775168 | bytes 16797696 | tf_op jit(solution)/shard_map/while/body/eval_jaxpr/vmap()/reduce_sum | solution.py:55
  487.4 1.4 copy.160
  488.9 7.1 %fusion.72 = (f32[2,64,2,8]{1,3,0,2:T(8,128)S(1)}, f32[2,2048,2,64,8]{1,3,4,2,0:T(8,128)}) fusion(pred[2,2048]{1,0:T(4,128)(4,1)S(1)} %compare_bitcast_fusion.2, bf16[2048,2,128,1,1]{0,2,4,3,1:T(8,128)(2,1)S(1)} %bitcast.138, bf16[2,64,2,8,128]{4,3,2,1,0:T(8,128)(2,1)S(1)} %dynamic-slice_bitcast_fusion.2), kind=kOutput, calls=%fused_computation.9.clone.1 | convolution fusion | flops 1086322688 | bytes 18362368 | tf_op jit(solution)/shard_map/while/body/eval_jaxpr/vmap(tkgd,lkd->tkgl)/dot_general | solution.py:49
  496.0 7.6 %fusion.73 = f32[2,64,2,8,128]{4,1,3,0,2:T(8,128)S(1)} fusion(bf16[2048,2,128,1,1]{0,2,4,3,1:T(8,128)(2,1)S(1)} %bitcast.142, f32[2,2048,2,64,8]{1,3,4,2,0:T(8,128)} %get-tuple-element.170, f32[2,64,2,8]{1,3,0,2:T(8,128)S(1)} %get-tuple-element.171, pred[2,2048]{1,0:T(4,128)(4,1)S(1)} %compare_bitcast_fusion.2), kind=kOutput, calls=%fused_computation.12.clone.1 | convolution fusion | flops 1090519040 | bytes 18886656 | tf_op jit(solution)/shard_map/while/body/eval_jaxpr/vmap(tkgl,lkd->tkgd)/dot_general | solution.py:58
  503.6 7.8 %fusion.74 = f32[2,64,2,8]{1,3,0,2:T(8,128)S(1)} fusion(f32[2,2048,2,64,8]{1,3,4,2,0:T(8,128)} %get-tuple-element.170, f32[2,64,2,8]{1,3,0,2:T(8,128)S(1)} %get-tuple-element.171, pred[2,2048]{1,0:T(4,128)(4,1)S(1)} %compare_bitcast_fusion.2), kind=kLoop, calls=%fused_computation.7.clone.1 | loop fusion | flops 16775168 | bytes 16797696 | tf_op jit(solution)/shard_map/while/body/eval_jaxpr/vmap()/reduce_sum | solution.py:55
  517.6 1.4 copy.160
  519.0 7.1 %fusion.72 = (f32[2,64,2,8]{1,3,0,2:T(8,128)S(1)}, f32[2,2048,2,64,8]{1,3,4,2,0:T(8,128)}) fusion(pred[2,2048]{1,0:T(4,128)(4,1)S(1)} %compare_bitcast_fusion.2, bf16[2048,2,128,1,1]{0,2,4,3,1:T(8,128)(2,1)S(1)} %bitcast.138, bf16[2,64,2,8,128]{4,3,2,1,0:T(8,128)(2,1)S(1)} %dynamic-slice_bitcast_fusion.2), kind=kOutput, calls=%fused_computation.9.clone.1 | convolution fusion | flops 1086322688 | bytes 18362368 | tf_op jit(solution)/shard_map/while/body/eval_jaxpr/vmap(tkgd,lkd->tkgl)/dot_general | solution.py:49
  526.1 7.6 %fusion.73 = f32[2,64,2,8,128]{4,1,3,0,2:T(8,128)S(1)} fusion(bf16[2048,2,128,1,1]{0,2,4,3,1:T(8,128)(2,1)S(1)} %bitcast.142, f32[2,2048,2,64,8]{1,3,4,2,0:T(8,128)} %get-tuple-element.170, f32[2,64,2,8]{1,3,0,2:T(8,128)S(1)} %get-tuple-element.171, pred[2,2048]{1,0:T(4,128)(4,1)S(1)} %compare_bitcast_fusion.2), kind=kOutput, calls=%fused_computation.12.clone.1 | convolution fusion | flops 1090519040 | bytes 18886656 | tf_op jit(solution)/shard_map/while/body/eval_jaxpr/vmap(tkgl,lkd->tkgd)/dot_general | solution.py:58
  533.7 7.8 %fusion.74 = f32[2,64,2,8]{1,3,0,2:T(8,128)S(1)} fusion(f32[2,2048,2,64,8]{1,3,4,2,0:T(8,128)} %get-tuple-element.170, f32[2,64,2,8]{1,3,0,2:T(8,128)S(1)} %get-tuple-element.171, pred[2,2048]{1,0:T(4,128)(4,1)S(1)} %compare_bitcast_fusion.2), kind=kLoop, calls=%fused_computation.7.clone.1 | loop fusion | flops 16775168 | bytes 16797696 | tf_op jit(solution)/shard_map/while/body/eval_jaxpr/vmap()/reduce_sum | solution.py:55
  549.2 7.1 %fusion.72 = (f32[2,64,2,8]{1,3,0,2:T(8,128)S(1)}, f32[2,2048,2,64,8]{1,3,4,2,0:T(8,128)}) fusion(pred[2,2048]{1,0:T(4,128)(4,1)S(1)} %compare_bitcast_fusion.2, bf16[2048,2,128,1,1]{0,2,4,3,1:T(8,128)(2,1)S(1)} %bitcast.138, bf16[2,64,2,8,128]{4,3,2,1,0:T(8,128)(2,1)S(1)} %dynamic-slice_bitcast_fusion.2), kind=kOutput, calls=%fused_computation.9.clone.1 | convolution fusion | flops 1086322688 | bytes 18362368 | tf_op jit(solution)/shard_map/while/body/eval_jaxpr/vmap(tkgd,lkd->tkgl)/dot_general | solution.py:49
  556.3 7.6 %fusion.73 = f32[2,64,2,8,128]{4,1,3,0,2:T(8,128)S(1)} fusion(bf16[2048,2,128,1,1]{0,2,4,3,1:T(8,128)(2,1)S(1)} %bitcast.142, f32[2,2048,2,64,8]{1,3,4,2,0:T(8,128)} %get-tuple-element.170, f32[2,64,2,8]{1,3,0,2:T(8,128)S(1)} %get-tuple-element.171, pred[2,2048]{1,0:T(4,128)(4,1)S(1)} %compare_bitcast_fusion.2), kind=kOutput, calls=%fused_computation.12.clone.1 | convolution fusion | flops 1090519040 | bytes 18886656 | tf_op jit(solution)/shard_map/while/body/eval_jaxpr/vmap(tkgl,lkd->tkgd)/dot_general | solution.py:58
  563.9 7.8 %fusion.74 = f32[2,64,2,8]{1,3,0,2:T(8,128)S(1)} fusion(f32[2,2048,2,64,8]{1,3,4,2,0:T(8,128)} %get-tuple-element.170, f32[2,64,2,8]{1,3,0,2:T(8,128)S(1)} %get-tuple-element.171, pred[2,2048]{1,0:T(4,128)(4,1)S(1)} %compare_bitcast_fusion.2), kind=kLoop, calls=%fused_computation.7.clone.1 | loop fusion | flops 16775168 | bytes 16797696 | tf_op jit(solution)/shard_map/while/body/eval_jaxpr/vmap()/reduce_sum | solution.py:55
  578.0 1.4 copy.160
  579.4 7.1 %fusion.72 = (f32[2,64,2,8]{1,3,0,2:T(8,128)S(1)}, f32[2,2048,2,64,8]{1,3,4,2,0:T(8,128)}) fusion(pred[2,2048]{1,0:T(4,128)(4,1)S(1)} %compare_bitcast_fusion.2, bf16[2048,2,128,1,1]{0,2,4,3,1:T(8,128)(2,1)S(1)} %bitcast.138, bf16[2,64,2,8,128]{4,3,2,1,0:T(8,128)(2,1)S(1)} %dynamic-slice_bitcast_fusion.2), kind=kOutput, calls=%fused_computation.9.clone.1 | convolution fusion | flops 1086322688 | bytes 18362368 | tf_op jit(solution)/shard_map/while/body/eval_jaxpr/vmap(tkgd,lkd->tkgl)/dot_general | solution.py:49
  586.5 7.6 %fusion.73 = f32[2,64,2,8,128]{4,1,3,0,2:T(8,128)S(1)} fusion(bf16[2048,2,128,1,1]{0,2,4,3,1:T(8,128)(2,1)S(1)} %bitcast.142, f32[2,2048,2,64,8]{1,3,4,2,0:T(8,128)} %get-tuple-element.170, f32[2,64,2,8]{1,3,0,2:T(8,128)S(1)} %get-tuple-element.171, pred[2,2048]{1,0:T(4,128)(4,1)S(1)} %compare_bitcast_fusion.2), kind=kOutput, calls=%fused_computation.12.clone.1 | convolution fusion | flops 1090519040 | bytes 18886656 | tf_op jit(solution)/shard_map/while/body/eval_jaxpr/vmap(tkgl,lkd->tkgd)/dot_general | solution.py:58
  594.1 7.8 %fusion.74 = f32[2,64,2,8]{1,3,0,2:T(8,128)S(1)} fusion(f32[2,2048,2,64,8]{1,3,4,2,0:T(8,128)} %get-tuple-element.170, f32[2,64,2,8]{1,3,0,2:T(8,128)S(1)} %get-tuple-element.171, pred[2,2048]{1,0:T(4,128)(4,1)S(1)} %compare_bitcast_fusion.2), kind=kLoop, calls=%fused_computation.7.clone.1 | loop fusion | flops 16775168 | bytes 16797696 | tf_op jit(solution)/shard_map/while/body/eval_jaxpr/vmap()/reduce_sum | solution.py:55
  609.6 7.1 %fusion.72 = (f32[2,64,2,8]{1,3,0,2:T(8,128)S(1)}, f32[2,2048,2,64,8]{1,3,4,2,0:T(8,128)}) fusion(pred[2,2048]{1,0:T(4,128)(4,1)S(1)} %compare_bitcast_fusion.2, bf16[2048,2,128,1,1]{0,2,4,3,1:T(8,128)(2,1)S(1)} %bitcast.138, bf16[2,64,2,8,128]{4,3,2,1,0:T(8,128)(2,1)S(1)} %dynamic-slice_bitcast_fusion.2), kind=kOutput, calls=%fused_computation.9.clone.1 | convolution fusion | flops 1086322688 | bytes 18362368 | tf_op jit(solution)/shard_map/while/body/eval_jaxpr/vmap(tkgd,lkd->tkgl)/dot_general | solution.py:49
  616.7 7.6 %fusion.73 = f32[2,64,2,8,128]{4,1,3,0,2:T(8,128)S(1)} fusion(bf16[2048,2,128,1,1]{0,2,4,3,1:T(8,128)(2,1)S(1)} %bitcast.142, f32[2,2048,2,64,8]{1,3,4,2,0:T(8,128)} %get-tuple-element.170, f32[2,64,2,8]{1,3,0,2:T(8,128)S(1)} %get-tuple-element.171, pred[2,2048]{1,0:T(4,128)(4,1)S(1)} %compare_bitcast_fusion.2), kind=kOutput, calls=%fused_computation.12.clone.1 | convolution fusion | flops 1090519040 | bytes 18886656 | tf_op jit(solution)/shard_map/while/body/eval_jaxpr/vmap(tkgl,lkd->tkgd)/dot_general | solution.py:58
  624.3 7.8 %fusion.74 = f32[2,64,2,8]{1,3,0,2:T(8,128)S(1)} fusion(f32[2,2048,2,64,8]{1,3,4,2,0:T(8,128)} %get-tuple-element.170, f32[2,64,2,8]{1,3,0,2:T(8,128)S(1)} %get-tuple-element.171, pred[2,2048]{1,0:T(4,128)(4,1)S(1)} %compare_bitcast_fusion.2), kind=kLoop, calls=%fused_computation.7.clone.1 | loop fusion | flops 16775168 | bytes 16797696 | tf_op jit(solution)/shard_map/while/body/eval_jaxpr/vmap()/reduce_sum | solution.py:55
  639.7 7.1 %fusion.72 = (f32[2,64,2,8]{1,3,0,2:T(8,128)S(1)}, f32[2,2048,2,64,8]{1,3,4,2,0:T(8,128)}) fusion(pred[2,2048]{1,0:T(4,128)(4,1)S(1)} %compare_bitcast_fusion.2, bf16[2048,2,128,1,1]{0,2,4,3,1:T(8,128)(2,1)S(1)} %bitcast.138, bf16[2,64,2,8,128]{4,3,2,1,0:T(8,128)(2,1)S(1)} %dynamic-slice_bitcast_fusion.2), kind=kOutput, calls=%fused_computation.9.clone.1 | convolution fusion | flops 1086322688 | bytes 18362368 | tf_op jit(solution)/shard_map/while/body/eval_jaxpr/vmap(tkgd,lkd->tkgl)/dot_general | solution.py:49
  646.8 7.6 %fusion.73 = f32[2,64,2,8,128]{4,1,3,0,2:T(8,128)S(1)} fusion(bf16[2048,2,128,1,1]{0,2,4,3,1:T(8,128)(2,1)S(1)} %bitcast.142, f32[2,2048,2,64,8]{1,3,4,2,0:T(8,128)} %get-tuple-element.170, f32[2,64,2,8]{1,3,0,2:T(8,128)S(1)} %get-tuple-element.171, pred[2,2048]{1,0:T(4,128)(4,1)S(1)} %compare_bitcast_fusion.2), kind=kOutput, calls=%fused_computation.12.clone.1 | convolution fusion | flops 1090519040 | bytes 18886656 | tf_op jit(solution)/shard_map/while/body/eval_jaxpr/vmap(tkgl,lkd->tkgd)/dot_general | solution.py:58
  654.4 7.8 %fusion.74 = f32[2,64,2,8]{1,3,0,2:T(8,128)S(1)} fusion(f32[2,2048,2,64,8]{1,3,4,2,0:T(8,128)} %get-tuple-element.170, f32[2,64,2,8]{1,3,0,2:T(8,128)S(1)} %get-tuple-element.171, pred[2,2048]{1,0:T(4,128)(4,1)S(1)} %compare_bitcast_fusion.2), kind=kLoop, calls=%fused_computation.7.clone.1 | loop fusion | flops 16775168 | bytes 16797696 | tf_op jit(solution)/shard_map/while/body/eval_jaxpr/vmap()/reduce_sum | solution.py:55
  664.8 4.2 gather_fusion.2
  673.1 4.4 fusion.16
  (194 shorter events, 74.4 us)
Async XLA Ops:
  6.5 2.8 copy-start.8
  6.5 2.8 copy-start.9
  6.5 40.8 %all-gather.8.cloned.1.call-start = ((), (), s32[]{:S(2)}) async-start(), calls=%async_computation.1 | async-start | bytes 2621440 | tf_op jit(solution)/shard_map/all_gather | solution.py:104
  7.3 70.8 %all-gather.12.cloned.1.call-start = ((), (), s32[]{:S(2)}) async-start(), calls=%async_computation.3 | async-start | bytes 2359296 | tf_op jit(solution)/shard_map/all_gather | solution.py:113
  8.0 100.2 %all-gather.14.cloned.1.call-start = ((), (), s32[]{:S(2)}) async-start(), calls=%async_computation.4 | async-start | bytes 2359296 | tf_op jit(solution)/shard_map/all_gather | solution.py:118
  8.7 251.6 %all-gather.10.cloned.1.call-start = ((), (), s32[]{:S(2)}) async-start(), calls=%async_computation.2 | async-start | bytes 18874368 | tf_op jit(solution)/shard_map/all_gather | solution.py:108
  9.3 401.8 %all-gather.6.cloned.1.call-start = ((), (), s32[]{:S(2)}) async-start(), calls=%async_computation | async-start | bytes 18874368 | tf_op jit(solution)/shard_map/all_gather | solution.py:16
  10.8 0.7 copy-start.18
  10.9 3.3 copy-start
  10.9 67.1 %copy-start.19 = (f32[4096]{0:T(1024)S(1)}, f32[4096]{0:T(1024)}, u32[]{:S(2)}) copy-start(f32[4096]{0:T(1024)} %param.17) | copy-start | bytes 49156
  10.9 67.1 %copy-start.21 = (f32[256]{0:T(256)S(1)}, f32[256]{0:T(256)}, u32[]{:S(2)}) copy-start(f32[256]{0:T(256)} %param.22) | copy-start | bytes 3076
  11.7 0.6 copy-start.12
  13.2 3.2 copy-start.16
  47.3 30.7 %copy-start.7 = (bf16[256,4096]{1,0:T(8,128)(2,1)S(1)}, bf16[256,4096]{1,0:T(8,128)(2,1)}, u32[]{:S(2)}) copy-start(bf16[256,4096]{1,0:T(8,128)(2,1)} %all-gather.8.cloned.1.call-done) | copy-start | bytes 6291460
  49.5 58.7 %copy-start.22 = (f32[256]{0:T(256)S(1)}, f32[256]{0:T(256)}, u32[]{:S(2)}) copy-start(f32[256]{0:T(256)} %param.23) | copy-start | bytes 3076
  80.5 179.8 %copy-start.20 = (f32[2048]{0:T(1024)S(1)}, f32[2048]{0:T(1024)}, u32[]{:S(2)}) copy-start(f32[2048]{0:T(1024)} %param.21) | copy-start | bytes 24580
  269.7 1.3 copy-start.4
  269.7 2.3 copy-start.5
  274.4 1.4 copy-start.2
  283.9 3.0 copy-start.3
  292.1 130.4 %copy-start.10 = (f32[8,2,64,16]{2,3,1,0:T(8,128)S(1)}, f32[8,2,64,16]{2,3,1,0:T(8,128)}, u32[]{:S(2)}) copy-start(f32[8,2,64,16]{2,3,1,0:T(8,128)} %custom-call.12) | copy-start | bytes 196612
  292.1 130.4 %copy-start.11 = (f32[8,2,64,16]{2,3,1,0:T(8,128)S(1)}, f32[8,2,64,16]{2,3,1,0:T(8,128)}, u32[]{:S(2)}) copy-start(f32[8,2,64,16]{2,3,1,0:T(8,128)} %custom-call.11) | copy-start | bytes 196612
  428.5 7.1 %copy-start.1 = (bf16[1,2048,256]{1,2,0:T(8,128)(2,1)S(1)}, bf16[1,2048,256]{1,2,0:T(8,128)(2,1)}, u32[]{:S(2)}) copy-start(bf16[1,2048,256]{1,2,0:T(8,128)(2,1)} %copy.160) | copy-start | bytes 3145732 | tf_op jit(solution)/shard_map/while
  458.7 7.1 %copy-start.1 = (bf16[1,2048,256]{1,2,0:T(8,128)(2,1)S(1)}, bf16[1,2048,256]{1,2,0:T(8,128)(2,1)}, u32[]{:S(2)}) copy-start(bf16[1,2048,256]{1,2,0:T(8,128)(2,1)} %copy.160) | copy-start | bytes 3145732 | tf_op jit(solution)/shard_map/while
  488.9 7.1 %copy-start.1 = (bf16[1,2048,256]{1,2,0:T(8,128)(2,1)S(1)}, bf16[1,2048,256]{1,2,0:T(8,128)(2,1)}, u32[]{:S(2)}) copy-start(bf16[1,2048,256]{1,2,0:T(8,128)(2,1)} %copy.160) | copy-start | bytes 3145732 | tf_op jit(solution)/shard_map/while
  519.0 7.1 %copy-start.1 = (bf16[1,2048,256]{1,2,0:T(8,128)(2,1)S(1)}, bf16[1,2048,256]{1,2,0:T(8,128)(2,1)}, u32[]{:S(2)}) copy-start(bf16[1,2048,256]{1,2,0:T(8,128)(2,1)} %copy.160) | copy-start | bytes 3145732 | tf_op jit(solution)/shard_map/while
  549.2 7.1 %copy-start.1 = (bf16[1,2048,256]{1,2,0:T(8,128)(2,1)S(1)}, bf16[1,2048,256]{1,2,0:T(8,128)(2,1)}, u32[]{:S(2)}) copy-start(bf16[1,2048,256]{1,2,0:T(8,128)(2,1)} %copy.160) | copy-start | bytes 3145732 | tf_op jit(solution)/shard_map/while
  579.4 7.1 %copy-start.1 = (bf16[1,2048,256]{1,2,0:T(8,128)(2,1)S(1)}, bf16[1,2048,256]{1,2,0:T(8,128)(2,1)}, u32[]{:S(2)}) copy-start(bf16[1,2048,256]{1,2,0:T(8,128)(2,1)} %copy.160) | copy-start | bytes 3145732 | tf_op jit(solution)/shard_map/while
  609.6 7.1 %copy-start.1 = (bf16[1,2048,256]{1,2,0:T(8,128)(2,1)S(1)}, bf16[1,2048,256]{1,2,0:T(8,128)(2,1)}, u32[]{:S(2)}) copy-start(bf16[1,2048,256]{1,2,0:T(8,128)(2,1)} %copy.160) | copy-start | bytes 3145732 | tf_op jit(solution)/shard_map/while
  639.7 7.1 %copy-start.1 = (bf16[1,2048,256]{1,2,0:T(8,128)(2,1)S(1)}, bf16[1,2048,256]{1,2,0:T(8,128)(2,1)}, u32[]{:S(2)}) copy-start(bf16[1,2048,256]{1,2,0:T(8,128)(2,1)} %copy.160) | copy-start | bytes 3145732 | tf_op jit(solution)/shard_map/while
  664.8 4.9 copy-start.13
  664.8 4.9 copy-start.17
  671.5 1.6 copy-start.6
  671.5 1.6 copy-start.14
  671.5 1.6 copy-start.15
Sparse Core Ops, SparseCore 0:
  9.2 38.0 all-gather.7
  48.9 29.0 all-gather.11
  79.6 28.5 all-gather.13
  109.7 150.5 all-gather.9
  261.8 149.3 all-gather.5
